TPU v7x, 128 devices: a whole 4x4x4 slice. The times are simulated.
128 devices in a mesh: seq: 4 (over y_lo, core), blk: 32 (over x, y_hi, z).
Axes of the slice: x: 4, y: 4 (y_hi: 2, y_lo: 2; y = y_hi * 2 + y_lo), z: 4, core: 2. Of those that a mesh axis runs over, the one named last changes fastest.
Arguments:
- tokens: bfloat16 [32768, 8192], P(('seq', 'blk')), may hold values from -21 to 21
- query_weight: bfloat16 [8192, 1024], replicated, may hold values from -0.0625 to 0.0625
- key_weight: bfloat16 [8192, 128], replicated, may hold values from -0.0625 to 0.0625
- value_weight: bfloat16 [8192, 128], replicated, may hold values from -0.0625 to 0.0625
- doc_lengths: int32 [4, 4], replicated, may hold values from 1 to 4096, 8192 in all within a row
- slot_index: int32 [32768], P(('seq', 'blk')), may hold values from 0 to 32767, as said below
Outputs:
- attended: bfloat16 [32768, 1024], P(('seq', 'blk'))
Inputs may be any that keep to these rules, and one draw needn't show every extreme that they name: `slot_index`: each value appears exactly once. The 256 rows of one loader device put at most 3 rows into the 256 consecutive slots k * 256 to (k + 1) * 256 - 1 of any k, and exactly 3 into some of them.
All inputs are finite; a program needn't handle non-finite values.
Results may differ from a plain program's by a relative error of at most 0.0085.
The roundings to bfloat16 on the way count: a program that leaves them out, or rounds other values in their place, can miss the bound.
Values may be sent and summed in bfloat16 or wider, within the bound.
A program may use at most 128 MiB of HBM per device.

v0:
```python
import math
import jax
import jax.numpy as jnp
from jax import lax
from jax.sharding import PartitionSpec as P

HQ = 8
HS = 128


def rotate_pairs(values, positions):
    half_width = values.shape[-1] // 2
    frequency = 500000.0 ** (-(jnp.arange(half_width, dtype=jnp.float32) * 2.0 / values.shape[-1]))
    angles = positions.astype(jnp.float32)[:, None, None] * frequency[None, None, :]
    cosine = jnp.cos(angles)
    sine_values = jnp.sin(angles)
    leading = values[..., :half_width]
    trailing = values[..., half_width:]
    return jnp.concatenate(
        [leading * cosine - trailing * sine_values, trailing * cosine + leading * sine_values],
        axis=-1,
    )


def doc_positions(lengths_table, local_slot):
    doc_ends = jnp.cumsum(lengths_table, axis=-1)
    starts = doc_ends - lengths_table
    document = jnp.sum((local_slot[:, None] >= doc_ends).astype(jnp.int32), axis=1)
    picked = jnp.arange(lengths_table.shape[-1], dtype=jnp.int32)[None, :] == document[:, None]
    start_of = jnp.sum(jnp.where(picked, starts, 0), axis=1)
    return (document, local_slot - start_of)


def place_slot(local_slot, rows_dev):
    return (local_slot // rows_dev, local_slot % rows_dev)


def slot_of(device, row_index, rows_dev):
    return device * rows_dev + row_index


def project_rows(rows, query_weight, key_weight, value_weight):
    lead_shape = rows.shape[:-1]
    flat_rows = rows.reshape(-1, rows.shape[-1])
    results = []
    for weight in (query_weight, key_weight, value_weight):
        product = jnp.dot(flat_rows, weight, preferred_element_type=jnp.float32)
        results.append(product.reshape(lead_shape + (weight.shape[1],)))
    return (results[0], results[1], results[2])


def finish_rows(query_f, key_f, value_f, positions):
    row_count = query_f.shape[0]
    query_rows = (
        rotate_pairs(query_f.reshape(row_count, HQ, HS), positions)
        .reshape(row_count, HQ * HS)
        .astype(jnp.bfloat16)
    )
    key_rows = rotate_pairs(key_f[:, None, :], positions)[:, 0, :].astype(jnp.bfloat16)
    return (query_rows, key_rows, value_f.astype(jnp.bfloat16))


def arrange_rows(values, where_flat, rows_dev):
    width = values.shape[-1]
    empty = jnp.zeros((rows_dev, width), values.dtype)
    return empty.at[where_flat].set(values.reshape(-1, width), mode="drop")


def shards(tokens, query_weight, key_weight, value_weight, doc_lengths, slot_index):
    rows_dev = tokens.shape[0]
    device_count = lax.axis_size(("seq", "blk"))
    block_count = lax.axis_size("blk")
    group_rows = block_count * rows_dev
    capacity = rows_dev // device_count + 1
    seq_position = lax.axis_index("seq")
    block_position = lax.axis_index("blk")
    seq_count = doc_lengths.shape[0]
    group_of = slot_index // group_rows
    local_of = slot_index % group_rows
    target_block, target_row = place_slot(local_of, rows_dev)
    target = group_of * block_count + target_block
    same_target = target[:, None] == target[None, :]
    row_order = jnp.arange(rows_dev, dtype=jnp.int32)
    earlier = row_order[None, :] < row_order[:, None]
    rank = jnp.sum((same_target & earlier).astype(jnp.int32), axis=1)
    flat_index = target * capacity + rank
    where_send = (
        jnp.full((device_count * capacity,), rows_dev, jnp.int32).at[flat_index].set(target_row)
    )
    where_send = where_send.reshape(device_count, capacity)
    my_local = slot_of(block_position, row_order, rows_dev)
    group_pick = jnp.arange(seq_count, dtype=jnp.int32)[:, None] == seq_position
    my_lengths = jnp.sum(jnp.where(group_pick, doc_lengths, 0), axis=0)[None, :]
    my_doc, my_pos = doc_positions(my_lengths, my_local)
    outgoing = (
        jnp.zeros((device_count * capacity, tokens.shape[1]), jnp.bfloat16)
        .at[flat_index]
        .set(tokens)
    )
    outgoing = outgoing.reshape(device_count, capacity, tokens.shape[1])
    rows_in = lax.all_to_all(outgoing, ("seq", "blk"), split_axis=0, concat_axis=0, tiled=True)
    where_in = lax.all_to_all(where_send, ("seq", "blk"), split_axis=0, concat_axis=0, tiled=True)
    query_f, key_f, value_f = project_rows(rows_in, query_weight, key_weight, value_weight)
    query_f, key_f, value_f, where_recv = (query_f, key_f, value_f, where_in)
    where_flat = where_recv.reshape(-1)
    query_rows, key_rows, value_rows = finish_rows(
        arrange_rows(query_f, where_flat, rows_dev),
        arrange_rows(key_f, where_flat, rows_dev),
        arrange_rows(value_f, where_flat, rows_dev),
        my_pos,
    )
    query_three = query_rows.reshape(rows_dev, HQ, HS)
    score_scale = 1.0 / math.sqrt(HS)
    initial = (
        jnp.full((rows_dev, HQ), -1e30, jnp.float32),
        jnp.zeros((rows_dev, HQ), jnp.float32),
        jnp.zeros((rows_dev, HQ, HS), jnp.float32),
    )
    key_piece = lax.all_gather(key_rows, "blk", axis=0, tiled=True)
    value_piece = lax.all_gather(value_rows, "blk", axis=0, tiled=True)
    key_count = key_piece.shape[0]
    block_width = math.gcd(key_count, 512)
    gathered_rows = jnp.arange(key_count, dtype=jnp.int32)
    key_local = slot_of(gathered_rows // rows_dev, gathered_rows % rows_dev, rows_dev)
    key_doc, unused_pos = doc_positions(my_lengths, key_local)

    def one_block(block_number, running):
        offset = block_number * block_width
        key_block = lax.dynamic_slice_in_dim(key_piece, offset, block_width, 0)
        value_block = lax.dynamic_slice_in_dim(value_piece, offset, block_width, 0)
        local_block = lax.dynamic_slice_in_dim(key_local, offset, block_width, 0)
        doc_block = lax.dynamic_slice_in_dim(key_doc, offset, block_width, 0)
        allowed = (my_doc[:, None] == doc_block[None, :]) & (
            local_block[None, :] <= my_local[:, None]
        )

        def update(current):
            running_max, denominator, numerator = current
            scores = (
                jnp.einsum(
                    "qhd,kd->qhk", query_three, key_block, preferred_element_type=jnp.float32
                )
                * score_scale
            )
            allowed_three = allowed[:, None, :]
            scores = jnp.where(allowed_three, scores, -1e30)
            new_max = jnp.maximum(running_max, jnp.max(scores, axis=-1))
            weights = jnp.where(allowed_three, jnp.exp(scores - new_max[..., None]), 0.0)
            factor = jnp.exp(running_max - new_max)
            denominator = denominator * factor + jnp.sum(weights, axis=-1)
            numerator = numerator * factor[..., None] + jnp.einsum(
                "qhk,kd->qhd",
                weights.astype(jnp.bfloat16),
                value_block,
                preferred_element_type=jnp.float32,
            )
            return (new_max, denominator, numerator)

        def unchanged(current):
            return current

        return lax.cond(jnp.any(allowed), update, unchanged, running)

    final_max, denominator, numerator = lax.fori_loop(
        0, key_count // block_width, one_block, initial
    )
    attended_rows = (
        (numerator / denominator[..., None]).reshape(rows_dev, HQ * HS).astype(jnp.bfloat16)
    )
    is_filled = (where_flat < rows_dev).astype(jnp.bfloat16)
    returning = (
        jnp.take(attended_rows, jnp.minimum(where_flat, rows_dev - 1), axis=0) * is_filled[:, None]
    )
    returning = returning.reshape(device_count, capacity, HQ * HS)
    returned = lax.all_to_all(returning, ("seq", "blk"), split_axis=0, concat_axis=0, tiled=True)
    return jnp.take(returned.reshape(-1, HQ * HS), flat_index, axis=0)


def solution(mesh):
    in_specs = (P(("seq", "blk"), None), P(), P(), P(), P(), P(("seq", "blk")))
    out_specs = P(("seq", "blk"), None)
    return jax.shard_map(shards, mesh=mesh, in_specs=in_specs, out_specs=out_specs, check_vma=False)
```

profile of v0, /device:TPU:1, one launch (start us, length us, event | category | flops | bytes accessed | tf_op | source)
XLA Modules:
  0.0 446.0 jit_solution(17842980668918397970)
XLA Ops:
  6.5 0.8 and_select_fusion
  7.4 0.7 fusion.50
  8.3 1.4 scatter_custom_fusion
  9.7 0.8 all_to_all.12
  10.5 11.5 %all-to-all-start = ((s32[128,1,3]{2,1,0:T(1,128)}), s32[128,1,3]{2,1,0:T(1,128)S(1)}, u32[]{:S(2)}, u32[]{:S(2)}) async-start(s32[128,1,3]{2,1,0:T(1,128)} %bitcast.3), calls=%async_computation | async-start | bytes 131072 | tf_op jit(solution)/shard_map/all_to_all | solution.py:102
  22.0 11.3 %scatter_custom_fusion.1 = bf16[384,8192]{1,0:T(8,128)(2,1)} fusion(s32[256]{0:T(256)S(1)} %get-tuple-element.406, bf16[256,8192]{1,0:T(8,128)(2,1)} %param.10, bf16[]{:T(256)} %constant.190.clone.1), kind=kCustom, calls=%fused_computation.30 | custom fusion | bytes 6291968 | tf_op jit(solution)/shard_map/scatter | solution.py:98
  33.3 12.8 %reshape.294 = bf16[128,3,8192]{2,1,0:T(4,128)(2,1)} reshape(bf16[384,8192]{1,0:T(8,128)(2,1)} %scatter_custom_fusion.1) | data formatting | bytes 12582912 | tf_op jit(solution)/shard_map/reshape | solution.py:100
  46.1 10.2 %all-to-all-start.1 = ((bf16[128,3,8192]{2,1,0:T(4,128)(2,1)}), bf16[128,3,8192]{2,1,0:T(4,128)(2,1)}, u32[]{:S(2)}, u32[]{:S(2)}) async-start(bf16[128,3,8192]{2,1,0:T(4,128)(2,1)} %reshape.294), calls=%async_computation.1 | async-start | bytes 16777216 | tf_op jit(solution)/shard_map/all_to_all | solution.py:101
  57.6 0.8 broadcast_minimum_fusion
  58.7 105.3 %all-to-all-done.1 = bf16[128,3,8192]{2,1,0:T(4,128)(2,1)} async-done(((bf16[128,3,8192]{2,1,0:T(4,128)(2,1)}), bf16[128,3,8192]{2,1,0:T(4,128)(2,1)}, u32[]{:S(2)}, u32[]{:S(2)}) %all-to-all-start.1) | async-done | bytes 6291488 | tf_op jit(solution)/shard_map/all_to_all | solution.py:101
  164.0 13.8 %reshape.295 = bf16[384,8192]{1,0:T(8,128)(2,1)} reshape(bf16[128,3,8192]{2,1,0:T(4,128)(2,1)} %all-to-all-done.1) | data formatting | bytes 12582912 | tf_op jit(solution)/shard_map/reshape | solution.py:44
  177.8 4.6 %fusion.54 = f32[384,128]{1,0:T(8,128)S(1)} fusion(bf16[384,8192]{1,0:T(8,128)(2,1)} %reshape.295, bf16[8192,128]{1,0:T(8,128)(2,1)S(1)} %copy-done), kind=kOutput, calls=%fused_computation.115 | convolution fusion | flops 805306368 | bytes 8585216 | tf_op jit(solution)/shard_map/dot_general | solution.py:47
  182.3 1.5 scatter_custom_fusion.2
  184.9 5.2 %fusion.56 = f32[384,128]{1,0:T(8,128)S(1)} fusion(bf16[384,8192]{1,0:T(8,128)(2,1)} %reshape.295, bf16[8192,128]{1,0:T(8,128)(2,1)} %param.13), kind=kOutput, calls=%fused_computation.117 | convolution fusion | flops 805306368 | bytes 8585216 | tf_op jit(solution)/shard_map/dot_general | solution.py:47
  190.1 1.5 scatter_custom_fusion.4
  193.0 13.1 %fusion.55 = f32[384,1024]{1,0:T(8,128)} fusion(bf16[384,8192]{1,0:T(8,128)(2,1)} %reshape.295, bf16[8192,1024]{1,0:T(8,128)(2,1)} %param.11), kind=kOutput, calls=%fused_computation.116 | convolution fusion | flops 6442450944 | bytes 24641536 | tf_op jit(solution)/shard_map/dot_general | solution.py:47
  206.1 3.2 scatter_custom_fusion.3
  210.1 47.2 %all-gather.6.cloned.1.call-done = bf16[8192,1,128]{0,2,1:T(8,128)(2,1)} async-done(((bf16[256,1,128]{0,2,1:T(8,128)(2,1)}), bf16[8192,1,128]{0,2,1:T(8,128)(2,1)}) %all-gather.6.cloned.1.call-update) | async-done | bytes 2097168 | tf_op jit(solution)/shard_map/all_gather | solution.py:119
  257.3 4.1 copy.50
  261.4 69.5 %all-gather.4.cloned.1.call-done = bf16[8192,128]{1,0:T(8,128)(2,1)} async-done(((bf16[256,128]{1,0:T(8,128)(2,1)}), bf16[8192,128]{1,0:T(8,128)(2,1)}) %all-gather.4.cloned.1.call-update) | async-done | bytes 2097168 | tf_op jit(solution)/shard_map/all_gather | solution.py:120
  331.0 32.0 %while.18 = (s32[]{:T(128)}, f32[256,8]{0,1:T(8,128)S(1)}, f32[256,8]{0,1:T(8,128)S(1)}, f32[256,8,128]{2,0,1:T(8,128)S(1)}, s32[256]{0:T(256)S(1)}, /*index=5*/...) while((s32[]{:T(128)}, f32[256,8]{0,1:T(8,128)S(1)}, ...), condition=%wide.region_17.18_spmd.clone, body=%wide.region_11.17_spmd.clone.sunk | while | flops 551555328 | bytes 16138565 | solution.py:164
  331.1 0.8 fusion.66
  332.6 5.3 %conditional.3 = ((f32[256,8]{0,1:T(8,128)S(1)}, f32[256,8]{0,1:T(8,128)S(1)}, f32[256,8,128]{2,0,1:T(8,128)S(1)})) conditional(s32[]{:T(128)} %convert_element_type.80, (f32[256,8]{0,1:T(8,128)S(1)}, f32[256,8]{0,1:T(8,128)S(1)}, f32[256,8,128]{2,0,1:T(8,128)S(1)}) %tuple.65, (pred[256,512]{0,1:T(8,128)(4,1)S(1)}, bf16[8192,128]{1,0:T(8,128)(2,1)}, ...), branch_computations={%region_13.13_spmd, %region_14.16_spmd} | conditional | flops 551030784 | bytes 15991840 | solution.py:162
  332.6 1.7 fusion.2
  334.3 1.0 fusion.4
  335.4 2.5 fusion.8
  338.1 0.8 fusion.66
  339.8 0.8 fusion.66
  341.4 0.8 fusion.66
  343.1 0.8 fusion.66
  344.8 0.8 fusion.66
  346.4 0.8 fusion.66
  348.1 0.8 fusion.66
  349.8 0.8 fusion.66
  351.4 0.8 fusion.66
  353.1 0.8 fusion.66
  354.8 0.8 fusion.66
  356.5 0.8 fusion.66
  358.1 0.8 fusion.66
  359.8 0.8 fusion.66
  361.5 0.8 fusion.66
  363.3 2.1 gather_fusion
  365.9 1.7 select_multiply_fusion
  367.7 48.5 %all-to-all-start.2 = ((bf16[128,3,1024]{2,1,0:T(4,128)(2,1)}), bf16[128,3,1024]{2,1,0:T(4,128)(2,1)}, u32[]{:S(2)}, u32[]{:S(2)}) async-start(bf16[128,3,1024]{2,1,0:T(4,128)(2,1)} %select_multiply_fusion), calls=%async_computation.2 | async-start | bytes 2097152 | tf_op jit(solution)/shard_map/all_to_all | solution.py:175
  416.1 18.5 %all-to-all-done.2 = bf16[128,3,1024]{2,1,0:T(4,128)(2,1)} async-done(((bf16[128,3,1024]{2,1,0:T(4,128)(2,1)}), bf16[128,3,1024]{2,1,0:T(4,128)(2,1)}, u32[]{:S(2)}, u32[]{:S(2)}) %all-to-all-start.2) | async-done | bytes 786464 | tf_op jit(solution)/shard_map/all_to_all | solution.py:175
  434.7 2.4 reshape.297
  437.1 1.2 gather_fusion.1
  438.3 0.9 broadcast_select_fusion
  (113 shorter events, 8.5 us)
Async XLA Ops:
  6.5 171.2 %copy-start = (bf16[8192,128]{1,0:T(8,128)(2,1)S(1)}, bf16[8192,128]{1,0:T(8,128)(2,1)}, u32[]{:S(2)}) copy-start(bf16[8192,128]{1,0:T(8,128)(2,1)} %param.12) | copy-start | bytes 6291460
  10.5 35.6 %all-to-all-start = ((s32[128,1,3]{2,1,0:T(1,128)}), s32[128,1,3]{2,1,0:T(1,128)S(1)}, u32[]{:S(2)}, u32[]{:S(2)}) async-start(s32[128,1,3]{2,1,0:T(1,128)} %bitcast.3), calls=%async_computation | async-start | bytes 131072 | tf_op jit(solution)/shard_map/all_to_all | solution.py:102
  46.1 10.5 %copy-start.2 = (s32[4,4]{1,0:T(4,128)S(1)}, s32[4,4]{1,0:T(4,128)}, u32[]{:S(2)}) copy-start(s32[4,4]{1,0:T(4,128)} %param.14) | copy-start | bytes 196
  46.1 117.9 %all-to-all-start.1 = ((bf16[128,3,8192]{2,1,0:T(4,128)(2,1)}), bf16[128,3,8192]{2,1,0:T(4,128)(2,1)}, u32[]{:S(2)}, u32[]{:S(2)}) async-start(bf16[128,3,8192]{2,1,0:T(4,128)(2,1)} %reshape.294), calls=%async_computation.1 | async-start | bytes 16777216 | tf_op jit(solution)/shard_map/all_to_all | solution.py:101
  56.3 201.0 %all-gather.6.cloned.1.call-start = ((), (), s32[]{:S(2)}) async-start(), calls=%async_computation.4 | async-start | bytes 2162688 | tf_op jit(solution)/shard_map/all_gather | solution.py:119
  184.9 146.0 %all-gather.4.cloned.1.call-start = ((), (), s32[]{:S(2)}) async-start(), calls=%async_computation.3 | async-start | bytes 2162688 | tf_op jit(solution)/shard_map/all_gather | solution.py:120
  367.7 67.0 %all-to-all-start.2 = ((bf16[128,3,1024]{2,1,0:T(4,128)(2,1)}), bf16[128,3,1024]{2,1,0:T(4,128)(2,1)}, u32[]{:S(2)}, u32[]{:S(2)}) async-start(bf16[128,3,1024]{2,1,0:T(4,128)(2,1)} %select_multiply_fusion), calls=%async_computation.2 | async-start | bytes 2097152 | tf_op jit(solution)/shard_map/all_to_all | solution.py:175
  416.1 23.0 %copy-start.1 = (bf16[8192,128]{1,0:T(8,128)(2,1)S(1)}, bf16[8192,128]{1,0:T(8,128)(2,1)}, u32[]{:S(2)}) copy-start(bf16[8192,128]{1,0:T(8,128)(2,1)} %param.12) | copy-start | bytes 6291460
Sparse Core Ops, SparseCore 0:
  185.0 72.2 all-gather.5
  260.4 70.3 all-gather.3
where the time goes:
time: 448 us; the launch traced here: 446 us
  waiting for transfers between devices  241 us (54%)
  starting transfers between devices  70.4 us (16%)
  local copies, waits for them, and re-layouts  60.6 us (14%)
  matrix products  27.1 us (6%)
  other arithmetic  23 us (5%)
  between operations  13.7 us (3%)
  loops' own time  10.7 us (2%)
    all_to_all x1, waiting for transfers between devices, shards(): lax.all_to_all(outgoing, ('seq', 'blk'), split_axis=0, concat_axis=0, til...  105 us
    all_gather x1, waiting for transfers between devices, shards(): value_piece = lax.all_gather(value_rows, 'blk', axis=0, tiled=True)  69.5 us
    all_to_all x1, starting transfers between devices, shards(): lax.all_to_all(returning, ('seq', 'blk'), split_axis=0, concat_axis=0, ti...  48.5 us
    all_gather x1, waiting for transfers between devices, shards(): key_piece = lax.all_gather(key_rows, 'blk', axis=0, tiled=True)  47.2 us
    dot_general x3, matrix products, project_rows(): product = jnp.dot(flat_rows, weight, preferred_element_type=jnp.float32)  22.9 us
    all_to_all x1, waiting for transfers between devices, shards(): lax.all_to_all(returning, ('seq', 'blk'), split_axis=0, concat_axis=0, ti...  18.5 us
    reshape x1, local copies, waits for them, and re-layouts, project_rows(): flat_rows = rows.reshape(-1, rows.shape[-1])  13.8 us
    reduce_or x16, other arithmetic, one_block(): return lax.cond(jnp.any(allowed), update, unchanged, running)  13.6 us
  transfers between devices with their start and end apart: 5, of which 4 were waited for; matrix products, arithmetic and copies ran while one was open for 12% of the time, Pallas kernels for 0%

commit v1 on v0

--- a/solution.py
+++ b/solution.py
@@ -116,7 +116,9 @@
         jnp.zeros((rows_dev, HQ), jnp.float32),
         jnp.zeros((rows_dev, HQ, HS), jnp.float32),
     )
-    key_piece = lax.all_gather(key_rows, "blk", axis=0, tiled=True)
+    key_piece = jnp.concatenate(
+        lax.all_to_all(jnp.stack([key_rows] * lax.axis_size("blk")), "blk", 0, 0), axis=0
+    )
     value_piece = lax.all_gather(value_rows, "blk", axis=0, tiled=True)
     key_count = key_piece.shape[0]
     block_width = math.gcd(key_count, 512)

time: 448 us -> 395 us (0.88)
  waiting for transfers between devices: 241 us -> 180 us
  starting transfers between devices: 70.4 us -> 80.8 us
    all_gather x1 -> x0, waiting for transfers between devices: 47.2 us -> none  [shards(): key_piece = lax.all_gather(key_rows, 'blk', axis=0, tiled=True)]
    all_gather x1, waiting for transfers between devices: 69.5 us -> 47.8 us  [shards(): value_piece = lax.all_gather(value_rows, 'blk', axis=0, tiled=True)]
    all_to_all x0 -> x1, starting transfers between devices: none -> 10.4 us  [shards(): lax.all_to_all(jnp.stack([key_rows] * lax.axis_size('blk')), 'blk', 0, 0)]
    all_to_all x0 -> x1, waiting for transfers between devices: none -> 8.52 us  [shards(): lax.all_to_all(jnp.stack([key_rows] * lax.axis_size('blk')), 'blk', 0, 0)]
  transfers between devices with their start and end apart: 5 -> 5, of which waited for: 4 -> 4; matrix products, arithmetic and copies ran while one was open for 12% -> 13% of each run, Pallas kernels for 0% -> 0%
where the time goes in v1:
time: 395 us; the launch traced here: 393 us
  waiting for transfers between devices  180 us (46%)
  starting transfers between devices  80.8 us (20%)
  local copies, waits for them, and re-layouts  58.4 us (15%)
  matrix products  27.1 us (7%)
  other arithmetic  22.4 us (6%)
  between operations  13.7 us (3%)
  loops' own time  10.7 us (3%)
    all_to_all x1, waiting for transfers between devices, shards(): lax.all_to_all(outgoing, ('seq', 'blk'), split_axis=0, concat_axis=0, til...  105 us
    all_to_all x1, starting transfers between devices, shards(): lax.all_to_all(returning, ('seq', 'blk'), split_axis=0, concat_axis=0, ti...  48.5 us
    all_gather x1, waiting for transfers between devices, shards(): value_piece = lax.all_gather(value_rows, 'blk', axis=0, tiled=True)  47.8 us
    dot_general x3, matrix products, project_rows(): product = jnp.dot(flat_rows, weight, preferred_element_type=jnp.float32)  22.9 us
    all_to_all x1, waiting for transfers between devices, shards(): lax.all_to_all(returning, ('seq', 'blk'), split_axis=0, concat_axis=0, ti...  18.5 us
    reshape x1, local copies, waits for them, and re-layouts, project_rows(): flat_rows = rows.reshape(-1, rows.shape[-1])  13.8 us
    reduce_or x16, other arithmetic, one_block(): return lax.cond(jnp.any(allowed), update, unchanged, running)  13.6 us
    reshape x1, local copies, waits for them, and re-layouts, shards(): outgoing = outgoing.reshape(device_count, capacity, tokens.shape[1])  12.8 us
  transfers between devices with their start and end apart: 5, of which 4 were waited for; matrix products, arithmetic and copies ran while one was open for 13% of the time, Pallas kernels for 0%

profile of v1, /device:TPU:1, one launch (start us, length us, event | category | flops | bytes accessed | tf_op | source)
XLA Modules:
  0.0 393.2 jit_solution(1256144873318356759)
XLA Ops:
  6.5 0.8 and_select_fusion
  8.3 1.4 scatter_custom_fusion
  9.7 0.8 all_to_all.15
  10.5 11.5 %all-to-all-start = ((s32[128,1,3]{2,1,0:T(1,128)}), s32[128,1,3]{2,1,0:T(1,128)S(1)}, u32[]{:S(2)}, u32[]{:S(2)}) async-start(s32[128,1,3]{2,1,0:T(1,128)} %bitcast.3), calls=%async_computation | async-start | bytes 131072 | tf_op jit(solution)/shard_map/all_to_all | solution.py:102
  22.0 11.3 %scatter_custom_fusion.1 = bf16[384,8192]{1,0:T(8,128)(2,1)} fusion(s32[256]{0:T(256)S(1)} %get-tuple-element.406, bf16[256,8192]{1,0:T(8,128)(2,1)} %param.10, bf16[]{:T(256)} %constant.190.clone.1), kind=kCustom, calls=%fused_computation.30 | custom fusion | bytes 6291968 | tf_op jit(solution)/shard_map/scatter | solution.py:98
  33.3 12.8 %reshape.300 = bf16[128,3,8192]{2,1,0:T(4,128)(2,1)} reshape(bf16[384,8192]{1,0:T(8,128)(2,1)} %scatter_custom_fusion.1) | data formatting | bytes 12582912 | tf_op jit(solution)/shard_map/reshape | solution.py:100
  46.1 10.2 %all-to-all-start.1 = ((bf16[128,3,8192]{2,1,0:T(4,128)(2,1)}), bf16[128,3,8192]{2,1,0:T(4,128)(2,1)}, u32[]{:S(2)}, u32[]{:S(2)}) async-start(bf16[128,3,8192]{2,1,0:T(4,128)(2,1)} %reshape.300), calls=%async_computation.1 | async-start | bytes 16777216 | tf_op jit(solution)/shard_map/all_to_all | solution.py:101
  57.6 0.8 broadcast_minimum_fusion
  58.7 105.3 %all-to-all-done.1 = bf16[128,3,8192]{2,1,0:T(4,128)(2,1)} async-done(((bf16[128,3,8192]{2,1,0:T(4,128)(2,1)}), bf16[128,3,8192]{2,1,0:T(4,128)(2,1)}, u32[]{:S(2)}, u32[]{:S(2)}) %all-to-all-start.1) | async-done | bytes 6291488 | tf_op jit(solution)/shard_map/all_to_all | solution.py:101
  164.0 13.8 %reshape.301 = bf16[384,8192]{1,0:T(8,128)(2,1)} reshape(bf16[128,3,8192]{2,1,0:T(4,128)(2,1)} %all-to-all-done.1) | data formatting | bytes 12582912 | tf_op jit(solution)/shard_map/reshape | solution.py:44
  177.8 4.6 %fusion.56 = f32[384,128]{1,0:T(8,128)S(1)} fusion(bf16[384,8192]{1,0:T(8,128)(2,1)} %reshape.301, bf16[8192,128]{1,0:T(8,128)(2,1)S(1)} %copy-done), kind=kOutput, calls=%fused_computation.117 | convolution fusion | flops 805306368 | bytes 8585216 | tf_op jit(solution)/shard_map/dot_general | solution.py:47
  182.3 1.5 scatter_custom_fusion.4
  185.2 5.2 %fusion.54 = f32[384,128]{1,0:T(8,128)S(1)} fusion(bf16[384,8192]{1,0:T(8,128)(2,1)} %reshape.301, bf16[8192,128]{1,0:T(8,128)(2,1)} %param.12), kind=kOutput, calls=%fused_computation.115 | convolution fusion | flops 805306368 | bytes 8585216 | tf_op jit(solution)/shard_map/dot_general | solution.py:47
  190.4 1.5 scatter_custom_fusion.2
  192.5 1.8 stack.2
  194.3 10.4 %all-to-all-start.2 = ((bf16[32,256,128]{2,1,0:T(8,128)(2,1)}), bf16[32,256,128]{2,1,0:T(8,128)(2,1)}, u32[]{:S(2)}, u32[]{:S(2)}) async-start(bf16[32,256,128]{2,1,0:T(8,128)(2,1)} %stack.2), calls=%async_computation.2 | async-start | bytes 4194304 | tf_op jit(solution)/shard_map/all_to_all | solution.py:120
  204.7 13.1 %fusion.55 = f32[384,1024]{1,0:T(8,128)} fusion(bf16[384,8192]{1,0:T(8,128)(2,1)} %reshape.301, bf16[8192,1024]{1,0:T(8,128)(2,1)} %param.11), kind=kOutput, calls=%fused_computation.116 | convolution fusion | flops 6442450944 | bytes 24641536 | tf_op jit(solution)/shard_map/dot_general | solution.py:47
  217.8 3.2 scatter_custom_fusion.3
  221.8 8.5 %all-to-all-done.2 = bf16[32,256,128]{2,1,0:T(8,128)(2,1)} async-done(((bf16[32,256,128]{2,1,0:T(8,128)(2,1)}), bf16[32,256,128]{2,1,0:T(8,128)(2,1)}, u32[]{:S(2)}, u32[]{:S(2)}) %all-to-all-start.2) | async-done | bytes 2097184 | tf_op jit(solution)/shard_map/all_to_all | solution.py:120
  230.3 47.8 %all-gather.2.cloned.1.call-done = bf16[8192,128]{1,0:T(8,128)(2,1)} async-done(((bf16[256,128]{1,0:T(8,128)(2,1)}), bf16[8192,128]{1,0:T(8,128)(2,1)}) %all-gather.2.cloned.1.call-update) | async-done | bytes 2097168 | tf_op jit(solution)/shard_map/all_gather | solution.py:122
  278.2 32.0 %while.18 = (s32[]{:T(128)}, f32[256,8]{0,1:T(8,128)S(1)}, f32[256,8]{0,1:T(8,128)S(1)}, f32[256,8,128]{2,0,1:T(8,128)S(1)}, s32[256]{0:T(256)S(1)}, /*index=5*/...) while((s32[]{:T(128)}, f32[256,8]{0,1:T(8,128)S(1)}, ...), condition=%wide.region_17.18_spmd.clone, body=%wide.region_11.17_spmd.clone.sunk | while | flops 551555328 | bytes 16138565 | solution.py:166
  278.4 0.8 fusion.66
  279.9 5.3 %conditional.3 = ((f32[256,8]{0,1:T(8,128)S(1)}, f32[256,8]{0,1:T(8,128)S(1)}, f32[256,8,128]{2,0,1:T(8,128)S(1)})) conditional(s32[]{:T(128)} %convert_element_type.82, (f32[256,8]{0,1:T(8,128)S(1)}, f32[256,8]{0,1:T(8,128)S(1)}, f32[256,8,128]{2,0,1:T(8,128)S(1)}) %tuple.65, (pred[256,512]{0,1:T(8,128)(4,1)S(1)}, bf16[8192,128]{1,0:T(8,128)(2,1)}, ...), branch_computations={%region_13.13_spmd, %region_14.16_spmd} | conditional | flops 551030784 | bytes 15991840 | solution.py:164
  279.9 1.7 fusion.2
  281.6 1.0 fusion.4
  282.6 2.5 fusion.8
  285.3 0.8 fusion.66
  287.0 0.8 fusion.66
  288.7 0.8 fusion.66
  290.3 0.8 fusion.66
  292.0 0.8 fusion.66
  293.7 0.8 fusion.66
  295.3 0.8 fusion.66
  297.0 0.8 fusion.66
  298.7 0.8 fusion.66
  300.4 0.8 fusion.66
  302.0 0.8 fusion.66
  303.7 0.8 fusion.66
  305.4 0.8 fusion.66
  307.0 0.8 fusion.66
  308.7 0.8 fusion.66
  310.5 2.1 gather_fusion
  313.1 1.7 select_multiply_fusion
  314.9 48.5 %all-to-all-start.3 = ((bf16[128,3,1024]{2,1,0:T(4,128)(2,1)}), bf16[128,3,1024]{2,1,0:T(4,128)(2,1)}, u32[]{:S(2)}, u32[]{:S(2)}) async-start(bf16[128,3,1024]{2,1,0:T(4,128)(2,1)} %select_multiply_fusion), calls=%async_computation.3 | async-start | bytes 2097152 | tf_op jit(solution)/shard_map/all_to_all | solution.py:177
  363.4 18.5 %all-to-all-done.3 = bf16[128,3,1024]{2,1,0:T(4,128)(2,1)} async-done(((bf16[128,3,1024]{2,1,0:T(4,128)(2,1)}), bf16[128,3,1024]{2,1,0:T(4,128)(2,1)}, u32[]{:S(2)}, u32[]{:S(2)}) %all-to-all-start.3) | async-done | bytes 786464 | tf_op jit(solution)/shard_map/all_to_all | solution.py:177
  381.9 2.4 reshape.304
  384.3 1.2 gather_fusion.1
  385.5 0.9 broadcast_select_fusion
  (113 shorter events, 8.6 us)
Async XLA Ops:
  6.5 171.2 %copy-start = (bf16[8192,128]{1,0:T(8,128)(2,1)S(1)}, bf16[8192,128]{1,0:T(8,128)(2,1)}, u32[]{:S(2)}) copy-start(bf16[8192,128]{1,0:T(8,128)(2,1)} %param.13) | copy-start | bytes 6291460
  10.5 35.6 %all-to-all-start = ((s32[128,1,3]{2,1,0:T(1,128)}), s32[128,1,3]{2,1,0:T(1,128)S(1)}, u32[]{:S(2)}, u32[]{:S(2)}) async-start(s32[128,1,3]{2,1,0:T(1,128)} %bitcast.3), calls=%async_computation | async-start | bytes 131072 | tf_op jit(solution)/shard_map/all_to_all | solution.py:102
  46.1 10.5 %copy-start.2 = (s32[4,4]{1,0:T(4,128)S(1)}, s32[4,4]{1,0:T(4,128)}, u32[]{:S(2)}) copy-start(s32[4,4]{1,0:T(4,128)} %param.14) | copy-start | bytes 196
  46.1 117.9 %all-to-all-start.1 = ((bf16[128,3,8192]{2,1,0:T(4,128)(2,1)}), bf16[128,3,8192]{2,1,0:T(4,128)(2,1)}, u32[]{:S(2)}, u32[]{:S(2)}) async-start(bf16[128,3,8192]{2,1,0:T(4,128)(2,1)} %reshape.300), calls=%async_computation.1 | async-start | bytes 16777216 | tf_op jit(solution)/shard_map/all_to_all | solution.py:101
  56.3 221.8 %all-gather.2.cloned.1.call-start = ((), (), s32[]{:S(2)}) async-start(), calls=%async_computation.4 | async-start | bytes 2162688 | tf_op jit(solution)/shard_map/all_gather | solution.py:122
  194.3 36.0 %all-to-all-start.2 = ((bf16[32,256,128]{2,1,0:T(8,128)(2,1)}), bf16[32,256,128]{2,1,0:T(8,128)(2,1)}, u32[]{:S(2)}, u32[]{:S(2)}) async-start(bf16[32,256,128]{2,1,0:T(8,128)(2,1)} %stack.2), calls=%async_computation.2 | async-start | bytes 4194304 | tf_op jit(solution)/shard_map/all_to_all | solution.py:120
  314.9 67.0 %all-to-all-start.3 = ((bf16[128,3,1024]{2,1,0:T(4,128)(2,1)}), bf16[128,3,1024]{2,1,0:T(4,128)(2,1)}, u32[]{:S(2)}, u32[]{:S(2)}) async-start(bf16[128,3,1024]{2,1,0:T(4,128)(2,1)} %select_multiply_fusion), calls=%async_computation.3 | async-start | bytes 2097152 | tf_op jit(solution)/shard_map/all_to_all | solution.py:177
  363.3 23.0 %copy-start.1 = (bf16[8192,128]{1,0:T(8,128)(2,1)S(1)}, bf16[8192,128]{1,0:T(8,128)(2,1)}, u32[]{:S(2)}) copy-start(bf16[8192,128]{1,0:T(8,128)(2,1)} %param.13) | copy-start | bytes 6291460
Sparse Core Ops, SparseCore 0:
  184.6 93.4 all-gather.1
